TPU v7x, 256 devices: a whole 4x4x8 slice. The times are simulated.
256 devices in a mesh: sub: 4 (over x), row: 16 (over z, core), col: 4 (over y).
Axes of the slice: x: 4, y: 4, z: 8, core: 2. Of those that a mesh axis runs over, the one named last changes fastest.
Arguments:
- leaf_rhs: bfloat16 [4, 64, 4, 64, 256], P('sub', 'row', 'col'), may hold values from -6 to 6
- leaf_inverse: bfloat16 [4, 64, 4, 256, 256], P('sub', 'row', 'col'), may hold values from -0.5 to 0.5
- coupling: bfloat16 [4, 16, 64, 4, 256, 256], P('sub', 'row', None, 'col'), may hold values from -0.01171875 to 0.01171875
- pattern: int32 [4, 16, 64, 4], P('sub', 'row', None, 'col'), may hold values 0 or 1
- top_rhs: bfloat16 [16, 64, 256], replicated, may hold values from -6 to 6
- top_inverse: bfloat16 [16, 256, 256], replicated, may hold values from -0.5 to 0.5
- top_factor: bfloat16 [16, 16, 256, 256], P('row', 'col'), may hold values from -0.09375 to 0.09375
Outputs:
- leaf_solution: bfloat16 [4, 64, 4, 64, 256], P('sub', 'row', 'col')
- top_solution: bfloat16 [16, 64, 256], P('row')
All inputs are finite; a program needn't handle non-finite values. No bound on the sum of `pattern` on one device may be relied on, other than what follows from the above.
Results may differ from a plain program's by a relative error of at most 0.025.
Values may be sent and summed in bfloat16 or wider, within the bound.
No kernel may reach another device: no remote copies, remote signals or barrier semaphores. Data moves between devices by JAX's collectives and lax.ppermute only.
A program may use at most 128 MiB of HBM per device.

v0:
```python
import jax
import jax.numpy as jnp
from jax import lax
from jax.sharding import PartitionSpec as P


def spread(block, axis, source):
    block = jnp.where(lax.axis_index(axis) == source, block, jnp.zeros_like(block))
    return lax.psum(block, axis)


def local(leaf_rhs, leaf_inverse, coupling, pattern, top_rhs, top_inverse, top_factor):
    own_rhs = leaf_rhs[0, :, 0]
    own_inverse = jnp.tril(leaf_inverse[0, :, 0])
    coupled = coupling[0, :, :, 0]
    weights = pattern[0, :, :, 0].astype(jnp.bfloat16)
    blocks_row = coupled.shape[0]
    rhs_count = own_rhs.shape[1]
    block_size = own_rhs.shape[2]
    total_top = top_rhs.shape[0]
    leaf_forward = jnp.einsum(
        "inb,idb->ind", own_rhs, own_inverse, preferred_element_type=jnp.float32
    ).astype(jnp.bfloat16)
    block_slice = coupled
    weight_slice = weights
    scaled = (
        lax.all_gather(leaf_forward, "row", axis=0, tiled=True)[None]
        * weight_slice[:, :, None, None]
    )
    partial_value = jnp.einsum(
        "ainb,aieb->ane", scaled, block_slice, preferred_element_type=jnp.float32
    )
    updates = lax.psum(partial_value.astype(jnp.bfloat16), ("sub", "col")).astype(jnp.float32)
    row_start = lax.axis_index("row") * blocks_row
    full_row = lax.all_gather(top_factor, "col", axis=1, tiled=True)
    row_ids = row_start + jnp.arange(blocks_row)

    def forward_step(block_id, carried):
        pending, solved = carried
        local_row = jnp.clip(block_id - row_start, 0, blocks_row - 1)
        owner_row = block_id // blocks_row
        residue = (
            top_rhs[block_id].astype(jnp.float32) - updates[local_row] - pending[local_row]
        ).astype(jnp.bfloat16)
        solved_piece = jnp.dot(
            residue, jnp.tril(top_inverse[block_id]).T, preferred_element_type=jnp.float32
        ).astype(jnp.bfloat16)
        solved_piece = spread(solved_piece, "row", owner_row)
        column = lax.dynamic_index_in_dim(full_row, block_id, 1, keepdims=False)
        below = (row_ids > block_id).astype(jnp.float32)
        pending = pending + below[:, None, None] * jnp.einsum(
            "nb,aeb->ane", solved_piece, column, preferred_element_type=jnp.float32
        )
        solved = lax.dynamic_update_index_in_dim(solved, solved_piece, block_id, 0)
        return (pending, solved)

    start_state = (
        jnp.zeros((blocks_row, rhs_count, block_size), jnp.float32),
        jnp.zeros((total_top, rhs_count, block_size), jnp.bfloat16),
    )
    forward_all = lax.fori_loop(0, total_top, forward_step, start_state)[1]

    def backward_step(iteration, solved):
        block_id = total_top - 1 - iteration
        own_rows = lax.dynamic_slice_in_dim(solved, row_start, blocks_row, 0)
        above = (row_ids > block_id).astype(jnp.bfloat16)
        column = lax.dynamic_index_in_dim(full_row, block_id, 1, keepdims=False)
        term = jnp.einsum(
            "ane,aeb->nb",
            own_rows * above[:, None, None],
            column,
            preferred_element_type=jnp.float32,
        )
        summed = lax.psum(term.astype(jnp.bfloat16), "row").astype(jnp.float32)
        residue = (forward_all[block_id].astype(jnp.float32) - summed).astype(jnp.bfloat16)
        solved_piece = jnp.dot(
            residue, jnp.tril(top_inverse[block_id]), preferred_element_type=jnp.float32
        ).astype(jnp.bfloat16)
        return lax.dynamic_update_index_in_dim(solved, solved_piece, block_id, 0)

    solution = lax.fori_loop(
        0, total_top, backward_step, jnp.zeros((total_top, rhs_count, block_size), jnp.bfloat16)
    )
    own_top = lax.dynamic_slice_in_dim(solution, row_start, blocks_row, 0)
    block_slice = coupled
    weight_slice = weights
    scaled = own_top[:, None] * weight_slice[:, :, None, None]
    back_sums = lax.psum_scatter(
        jnp.einsum(
            "aine,aieb->inb", scaled, block_slice, preferred_element_type=jnp.float32
        ).astype(jnp.bfloat16),
        "row",
        scatter_dimension=0,
        tiled=True,
    ).astype(jnp.float32)
    leaf_residue = (leaf_forward.astype(jnp.float32) - back_sums).astype(jnp.bfloat16)
    leaf_result = jnp.einsum(
        "inb,ibd->ind", leaf_residue, own_inverse, preferred_element_type=jnp.float32
    ).astype(jnp.bfloat16)
    return (leaf_result[None, :, None], own_top)


def solution(mesh):
    placed = (
        P("sub", "row", "col", None, None),
        P("sub", "row", "col", None, None),
        P("sub", "row", None, "col", None, None),
        P("sub", "row", None, "col"),
        P(),
        P(),
        P("row", "col", None, None),
    )
    return jax.shard_map(
        local,
        mesh=mesh,
        in_specs=placed,
        out_specs=(P("sub", "row", "col", None, None), P("row", None, None)),
        check_vma=False,
    )
```

profile of v0, /device:TPU:4, one launch (start us, length us, event | category | flops | bytes accessed | tf_op | source)
XLA Modules:
  0.0 1736.7 jit_solution(8568360056786855845)
XLA Ops:
  59.8 62.8 %psum.35 = bf16[1,64,256]{2,1,0:T(8,128)(2,1)S(1)} all-reduce(bf16[1,64,256]{2,1,0:T(8,128)(2,1)S(1)} %fusion.62), channel_id=1, replica_groups=mesh['sub'=4,'row'=16,'col'=4] {'sub','col'}, use_global_device_ids=true, to_apply=%region_0.1 | all-reduce | flops 16384 | bytes 65536 | tf_op jit(solution)/shard_map/psum | solution.py:33
  122.7 768.0 %while.34 = (s32[]{:T(128)}, f32[1,64,256]{2,1,0:T(8,128)S(1)}, bf16[16,64,256]{2,1,0:T(8,128)(2,1)S(1)}, s32[1]{0:T(128)}, bf16[1,16,256,256]{3,2,1,0:T(8,128)(...) while((s32[]{:T(128)}, f32[1,64,256]{2,1,0:T(8,128)S(1)}, ...), condition=%wide.region_3.4_spmd.clone, body=%wide.region_1.3_spmd.clone.sunk | while | flops 17088520 | bytes 755900 | solution.py:61
  123.8 45.7 %psum.40 = bf16[64,256]{1,0:T(8,128)(2,1)S(1)} all-reduce(bf16[64,256]{1,0:T(8,128)(2,1)S(1)} %fusion.97), channel_id=1, replica_groups=mesh['sub'=4,'row'=16,'col'=4] {'row'}, use_global_device_ids=true, to_apply=%region_2.2 | all-reduce | flops 16384 | bytes 65536 | tf_op jit(solution)/shard_map/while/body/eval_jaxpr/psum | solution.py:9
  171.8 45.7 %psum.40 = bf16[64,256]{1,0:T(8,128)(2,1)S(1)} all-reduce(bf16[64,256]{1,0:T(8,128)(2,1)S(1)} %fusion.97), channel_id=1, replica_groups=mesh['sub'=4,'row'=16,'col'=4] {'row'}, use_global_device_ids=true, to_apply=%region_2.2 | all-reduce | flops 16384 | bytes 65536 | tf_op jit(solution)/shard_map/while/body/eval_jaxpr/psum | solution.py:9
  219.8 45.7 %psum.40 = bf16[64,256]{1,0:T(8,128)(2,1)S(1)} all-reduce(bf16[64,256]{1,0:T(8,128)(2,1)S(1)} %fusion.97), channel_id=1, replica_groups=mesh['sub'=4,'row'=16,'col'=4] {'row'}, use_global_device_ids=true, to_apply=%region_2.2 | all-reduce | flops 16384 | bytes 65536 | tf_op jit(solution)/shard_map/while/body/eval_jaxpr/psum | solution.py:9
  267.8 45.7 %psum.40 = bf16[64,256]{1,0:T(8,128)(2,1)S(1)} all-reduce(bf16[64,256]{1,0:T(8,128)(2,1)S(1)} %fusion.97), channel_id=1, replica_groups=mesh['sub'=4,'row'=16,'col'=4] {'row'}, use_global_device_ids=true, to_apply=%region_2.2 | all-reduce | flops 16384 | bytes 65536 | tf_op jit(solution)/shard_map/while/body/eval_jaxpr/psum | solution.py:9
  315.8 45.7 %psum.40 = bf16[64,256]{1,0:T(8,128)(2,1)S(1)} all-reduce(bf16[64,256]{1,0:T(8,128)(2,1)S(1)} %fusion.97), channel_id=1, replica_groups=mesh['sub'=4,'row'=16,'col'=4] {'row'}, use_global_device_ids=true, to_apply=%region_2.2 | all-reduce | flops 16384 | bytes 65536 | tf_op jit(solution)/shard_map/while/body/eval_jaxpr/psum | solution.py:9
  363.8 45.7 %psum.40 = bf16[64,256]{1,0:T(8,128)(2,1)S(1)} all-reduce(bf16[64,256]{1,0:T(8,128)(2,1)S(1)} %fusion.97), channel_id=1, replica_groups=mesh['sub'=4,'row'=16,'col'=4] {'row'}, use_global_device_ids=true, to_apply=%region_2.2 | all-reduce | flops 16384 | bytes 65536 | tf_op jit(solution)/shard_map/while/body/eval_jaxpr/psum | solution.py:9
  411.8 45.7 %psum.40 = bf16[64,256]{1,0:T(8,128)(2,1)S(1)} all-reduce(bf16[64,256]{1,0:T(8,128)(2,1)S(1)} %fusion.97), channel_id=1, replica_groups=mesh['sub'=4,'row'=16,'col'=4] {'row'}, use_global_device_ids=true, to_apply=%region_2.2 | all-reduce | flops 16384 | bytes 65536 | tf_op jit(solution)/shard_map/while/body/eval_jaxpr/psum | solution.py:9
  459.8 45.7 %psum.40 = bf16[64,256]{1,0:T(8,128)(2,1)S(1)} all-reduce(bf16[64,256]{1,0:T(8,128)(2,1)S(1)} %fusion.97), channel_id=1, replica_groups=mesh['sub'=4,'row'=16,'col'=4] {'row'}, use_global_device_ids=true, to_apply=%region_2.2 | all-reduce | flops 16384 | bytes 65536 | tf_op jit(solution)/shard_map/while/body/eval_jaxpr/psum | solution.py:9
  555.8 45.7 %psum.40 = bf16[64,256]{1,0:T(8,128)(2,1)S(1)} all-reduce(bf16[64,256]{1,0:T(8,128)(2,1)S(1)} %fusion.97), channel_id=1, replica_groups=mesh['sub'=4,'row'=16,'col'=4] {'row'}, use_global_device_ids=true, to_apply=%region_2.2 | all-reduce | flops 16384 | bytes 65536 | tf_op jit(solution)/shard_map/while/body/eval_jaxpr/psum | solution.py:9
  603.8 45.7 %psum.40 = bf16[64,256]{1,0:T(8,128)(2,1)S(1)} all-reduce(bf16[64,256]{1,0:T(8,128)(2,1)S(1)} %fusion.97), channel_id=1, replica_groups=mesh['sub'=4,'row'=16,'col'=4] {'row'}, use_global_device_ids=true, to_apply=%region_2.2 | all-reduce | flops 16384 | bytes 65536 | tf_op jit(solution)/shard_map/while/body/eval_jaxpr/psum | solution.py:9
  699.8 45.7 %psum.40 = bf16[64,256]{1,0:T(8,128)(2,1)S(1)} all-reduce(bf16[64,256]{1,0:T(8,128)(2,1)S(1)} %fusion.97), channel_id=1, replica_groups=mesh['sub'=4,'row'=16,'col'=4] {'row'}, use_global_device_ids=true, to_apply=%region_2.2 | all-reduce | flops 16384 | bytes 65536 | tf_op jit(solution)/shard_map/while/body/eval_jaxpr/psum | solution.py:9
  795.8 45.7 %psum.40 = bf16[64,256]{1,0:T(8,128)(2,1)S(1)} all-reduce(bf16[64,256]{1,0:T(8,128)(2,1)S(1)} %fusion.97), channel_id=1, replica_groups=mesh['sub'=4,'row'=16,'col'=4] {'row'}, use_global_device_ids=true, to_apply=%region_2.2 | all-reduce | flops 16384 | bytes 65536 | tf_op jit(solution)/shard_map/while/body/eval_jaxpr/psum | solution.py:9
  890.7 765.6 %while.33 = (s32[]{:T(128)}, bf16[16,64,256]{2,1,0:T(8,128)(2,1)S(1)}, bf16[16,64,256]{2,1,0:T(8,128)(2,1)S(1)}, s32[]{:T(128)}, s32[1]{0:T(128)}, /*index=5*/bf...) while((s32[]{:T(128)}, ...), condition=%wide.region_6.7_spmd, body=%wide.region_4.6_spmd.sunk | while | flops 17039368 | bytes 494251 | solution.py:81
  891.8 45.7 %psum.39 = bf16[64,256]{1,0:T(8,128)(2,1)S(1)} all-reduce(bf16[64,256]{1,0:T(8,128)(2,1)S(1)} %convolution_convert_fusion.6), channel_id=1, replica_groups=mesh['sub'=4,'row'=16,'col'=4] {'row'}, use_global_device_ids=true, to_apply=%region_5.5 | all-reduce | flops 16384 | bytes 65536 | tf_op jit(solution)/shard_map/while/body/eval_jaxpr/psum | solution.py:74
  939.6 45.7 %psum.39 = bf16[64,256]{1,0:T(8,128)(2,1)S(1)} all-reduce(bf16[64,256]{1,0:T(8,128)(2,1)S(1)} %convolution_convert_fusion.6), channel_id=1, replica_groups=mesh['sub'=4,'row'=16,'col'=4] {'row'}, use_global_device_ids=true, to_apply=%region_5.5 | all-reduce | flops 16384 | bytes 65536 | tf_op jit(solution)/shard_map/while/body/eval_jaxpr/psum | solution.py:74
  987.5 45.7 %psum.39 = bf16[64,256]{1,0:T(8,128)(2,1)S(1)} all-reduce(bf16[64,256]{1,0:T(8,128)(2,1)S(1)} %convolution_convert_fusion.6), channel_id=1, replica_groups=mesh['sub'=4,'row'=16,'col'=4] {'row'}, use_global_device_ids=true, to_apply=%region_5.5 | all-reduce | flops 16384 | bytes 65536 | tf_op jit(solution)/shard_map/while/body/eval_jaxpr/psum | solution.py:74
  1035.3 45.7 %psum.39 = bf16[64,256]{1,0:T(8,128)(2,1)S(1)} all-reduce(bf16[64,256]{1,0:T(8,128)(2,1)S(1)} %convolution_convert_fusion.6), channel_id=1, replica_groups=mesh['sub'=4,'row'=16,'col'=4] {'row'}, use_global_device_ids=true, to_apply=%region_5.5 | all-reduce | flops 16384 | bytes 65536 | tf_op jit(solution)/shard_map/while/body/eval_jaxpr/psum | solution.py:74
  1083.2 45.7 %psum.39 = bf16[64,256]{1,0:T(8,128)(2,1)S(1)} all-reduce(bf16[64,256]{1,0:T(8,128)(2,1)S(1)} %convolution_convert_fusion.6), channel_id=1, replica_groups=mesh['sub'=4,'row'=16,'col'=4] {'row'}, use_global_device_ids=true, to_apply=%region_5.5 | all-reduce | flops 16384 | bytes 65536 | tf_op jit(solution)/shard_map/while/body/eval_jaxpr/psum | solution.py:74
  1131.0 45.7 %psum.39 = bf16[64,256]{1,0:T(8,128)(2,1)S(1)} all-reduce(bf16[64,256]{1,0:T(8,128)(2,1)S(1)} %convolution_convert_fusion.6), channel_id=1, replica_groups=mesh['sub'=4,'row'=16,'col'=4] {'row'}, use_global_device_ids=true, to_apply=%region_5.5 | all-reduce | flops 16384 | bytes 65536 | tf_op jit(solution)/shard_map/while/body/eval_jaxpr/psum | solution.py:74
  1178.9 45.7 %psum.39 = bf16[64,256]{1,0:T(8,128)(2,1)S(1)} all-reduce(bf16[64,256]{1,0:T(8,128)(2,1)S(1)} %convolution_convert_fusion.6), channel_id=1, replica_groups=mesh['sub'=4,'row'=16,'col'=4] {'row'}, use_global_device_ids=true, to_apply=%region_5.5 | all-reduce | flops 16384 | bytes 65536 | tf_op jit(solution)/shard_map/while/body/eval_jaxpr/psum | solution.py:74
  1226.7 45.7 %psum.39 = bf16[64,256]{1,0:T(8,128)(2,1)S(1)} all-reduce(bf16[64,256]{1,0:T(8,128)(2,1)S(1)} %convolution_convert_fusion.6), channel_id=1, replica_groups=mesh['sub'=4,'row'=16,'col'=4] {'row'}, use_global_device_ids=true, to_apply=%region_5.5 | all-reduce | flops 16384 | bytes 65536 | tf_op jit(solution)/shard_map/while/body/eval_jaxpr/psum | solution.py:74
  1274.6 45.7 %psum.39 = bf16[64,256]{1,0:T(8,128)(2,1)S(1)} all-reduce(bf16[64,256]{1,0:T(8,128)(2,1)S(1)} %convolution_convert_fusion.6), channel_id=1, replica_groups=mesh['sub'=4,'row'=16,'col'=4] {'row'}, use_global_device_ids=true, to_apply=%region_5.5 | all-reduce | flops 16384 | bytes 65536 | tf_op jit(solution)/shard_map/while/body/eval_jaxpr/psum | solution.py:74
  1322.4 45.7 %psum.39 = bf16[64,256]{1,0:T(8,128)(2,1)S(1)} all-reduce(bf16[64,256]{1,0:T(8,128)(2,1)S(1)} %convolution_convert_fusion.6), channel_id=1, replica_groups=mesh['sub'=4,'row'=16,'col'=4] {'row'}, use_global_device_ids=true, to_apply=%region_5.5 | all-reduce | flops 16384 | bytes 65536 | tf_op jit(solution)/shard_map/while/body/eval_jaxpr/psum | solution.py:74
  1370.3 45.7 %psum.39 = bf16[64,256]{1,0:T(8,128)(2,1)S(1)} all-reduce(bf16[64,256]{1,0:T(8,128)(2,1)S(1)} %convolution_convert_fusion.6), channel_id=1, replica_groups=mesh['sub'=4,'row'=16,'col'=4] {'row'}, use_global_device_ids=true, to_apply=%region_5.5 | all-reduce | flops 16384 | bytes 65536 | tf_op jit(solution)/shard_map/while/body/eval_jaxpr/psum | solution.py:74
  1418.1 45.7 %psum.39 = bf16[64,256]{1,0:T(8,128)(2,1)S(1)} all-reduce(bf16[64,256]{1,0:T(8,128)(2,1)S(1)} %convolution_convert_fusion.6), channel_id=1, replica_groups=mesh['sub'=4,'row'=16,'col'=4] {'row'}, use_global_device_ids=true, to_apply=%region_5.5 | all-reduce | flops 16384 | bytes 65536 | tf_op jit(solution)/shard_map/while/body/eval_jaxpr/psum | solution.py:74
  1466.0 45.7 %psum.39 = bf16[64,256]{1,0:T(8,128)(2,1)S(1)} all-reduce(bf16[64,256]{1,0:T(8,128)(2,1)S(1)} %convolution_convert_fusion.6), channel_id=1, replica_groups=mesh['sub'=4,'row'=16,'col'=4] {'row'}, use_global_device_ids=true, to_apply=%region_5.5 | all-reduce | flops 16384 | bytes 65536 | tf_op jit(solution)/shard_map/while/body/eval_jaxpr/psum | solution.py:74
  1513.8 45.7 %psum.39 = bf16[64,256]{1,0:T(8,128)(2,1)S(1)} all-reduce(bf16[64,256]{1,0:T(8,128)(2,1)S(1)} %convolution_convert_fusion.6), channel_id=1, replica_groups=mesh['sub'=4,'row'=16,'col'=4] {'row'}, use_global_device_ids=true, to_apply=%region_5.5 | all-reduce | flops 16384 | bytes 65536 | tf_op jit(solution)/shard_map/while/body/eval_jaxpr/psum | solution.py:74
  1561.6 45.7 %psum.39 = bf16[64,256]{1,0:T(8,128)(2,1)S(1)} all-reduce(bf16[64,256]{1,0:T(8,128)(2,1)S(1)} %convolution_convert_fusion.6), channel_id=1, replica_groups=mesh['sub'=4,'row'=16,'col'=4] {'row'}, use_global_device_ids=true, to_apply=%region_5.5 | all-reduce | flops 16384 | bytes 65536 | tf_op jit(solution)/shard_map/while/body/eval_jaxpr/psum | solution.py:74
  1609.5 45.7 %psum.39 = bf16[64,256]{1,0:T(8,128)(2,1)S(1)} all-reduce(bf16[64,256]{1,0:T(8,128)(2,1)S(1)} %convolution_convert_fusion.6), channel_id=1, replica_groups=mesh['sub'=4,'row'=16,'col'=4] {'row'}, use_global_device_ids=true, to_apply=%region_5.5 | all-reduce | flops 16384 | bytes 65536 | tf_op jit(solution)/shard_map/while/body/eval_jaxpr/psum | solution.py:74
  1663.3 65.1 %reduce-scatter.2.cloned.1.call-done = bf16[4,64,256]{2,1,0:T(8,128)(2,1)} async-done(((bf16[64,64,256]{2,1,0:T(8,128)(2,1)}), bf16[4,64,256]{2,1,0:T(8,128)(2,1)}) %reduce-scatter.2.cloned.1.call-update) | async-done | bytes 131088 | tf_op jit(solution)/shard_map/reduce_scatter | solution.py:88
  (110 shorter events, 313.2 us)
Async XLA Ops:
  7.2 0.9 copy-start
  7.2 45.9 %all-gather.5.cloned.1.call-start = ((), (), s32[]{:S(2)}) async-start(), calls=%async_computation.2 | async-start | bytes 2228224 | tf_op jit(solution)/shard_map/all_gather | solution.py:27
  10.1 112.6 %all-gather.3.cloned.1.call-start = ((), (), s32[]{:S(2)}) async-start(), calls=%async_computation.1 | async-start | bytes 2621440 | tf_op jit(solution)/shard_map/all_gather | solution.py:35
  10.8 1717.5 %reduce-scatter.2.cloned.1.call-start = ((), (), s32[]{:S(2)}) async-start(), calls=%async_computation.3 | async-start | bytes 2228224 | tf_op jit(solution)/shard_map/reduce_scatter | solution.py:88
  1662.7 65.7 %copy-start.1 = (bf16[4,64,256]{2,1,0:T(8,128)(2,1)S(1)}, bf16[4,64,256]{2,1,0:T(8,128)(2,1)}, u32[]{:S(2)}) copy-start(bf16[4,64,256]{2,1,0:T(8,128)(2,1)} %fusion.50) | copy-start | bytes 393220
  1662.7 65.7 %copy-start.2 = (bf16[1,4,1,256,256]{4,3,2,1,0:T(8,128)(2,1)S(1)}, bf16[1,4,1,256,256]{4,3,2,1,0:T(8,128)(2,1)}, u32[]{:S(2)}) copy-start(bf16[1,4,1,256,256]{4,3,2,1,0:T(8,128)(2,1)} %param.12) | copy-start | bytes 1572868
Sparse Core Ops, SparseCore 0:
  10.4 42.6 all-gather.4
  54.9 32.1 all-gather.2
  1662.8 65.5 reduce-scatter.1
where the time goes:
time: 1740 us
  blocking collectives  1530 us (88%)
  waiting for transfers between devices  107 us (6%)
  matrix products  85.4 us (5%)
    psum x16, blocking collectives, backward_step(): summed = lax.psum(term.astype(jnp.bfloat16), 'row').astype(jnp.float32)  732 us
    psum x16, blocking collectives, spread(): return lax.psum(block, axis)  732 us
    reduce_scatter x1, waiting for transfers between devices, local(): lax.psum_scatter(jnp.einsum('aine,aieb->inb', scaled, block_slice, prefer...  65.1 us
    psum x1, blocking collectives, local(): lax.psum(partial_value.astype(jnp.bfloat16), ('sub', 'col'))  62.8 us
    all_gather x1, waiting for transfers between devices, local(): lax.all_gather(leaf_forward, 'row', axis=0, tiled=True)[None]  41.5 us
  transfers between devices with their start and end apart: 3, of which 2 were waited for; matrix products, arithmetic and copies ran while one was open for 0% of the time, Pallas kernels for 0%

commit v1 on v0

--- a/solution.py
+++ b/solution.py
@@ -4,9 +4,15 @@
 from jax.sharding import PartitionSpec as P
 
 
+def add_all(shard, name):
+    parts = lax.all_gather(shard, name, axis=0, tiled=False)
+    acc = parts.sum(axis=0)
+    return acc
+
+
 def spread(block, axis, source):
     block = jnp.where(lax.axis_index(axis) == source, block, jnp.zeros_like(block))
-    return lax.psum(block, axis)
+    return add_all(block, axis)
 
 
 def local(leaf_rhs, leaf_inverse, coupling, pattern, top_rhs, top_inverse, top_factor):

time: 1740 us -> 1280 us (0.74)
  blocking collectives: 1530 us -> 1060 us
    psum x16 -> x0, blocking collectives: 732 us -> none  [spread(): return lax.psum(block, axis)]
    all_gather x0 -> x16, blocking collectives: none -> 265 us  [add_all(): parts = lax.all_gather(shard, name, axis=0, tiled=False)]
  transfers between devices with their start and end apart: 3 -> 3, of which waited for: 2 -> 2; matrix products, arithmetic and copies ran while one was open for 0% -> 1% of each run, Pallas kernels for 0% -> 0%
where the time goes in v1:
time: 1280 us; the launch traced here: 1270 us
  blocking collectives  1060 us (83%)
  waiting for transfers between devices  108 us (8%)
  matrix products  85.5 us (7%)
  between operations  13.8 us (1%)
    psum x16, blocking collectives, backward_step(): summed = lax.psum(term.astype(jnp.bfloat16), 'row').astype(jnp.float32)  733 us
    all_gather x16, blocking collectives, add_all(): parts = lax.all_gather(shard, name, axis=0, tiled=False)  265 us
    reduce_scatter x1, waiting for transfers between devices, local(): lax.psum_scatter(jnp.einsum('aine,aieb->inb', scaled, block_slice, prefer...  65.3 us
    psum x1, blocking collectives, local(): lax.psum(partial_value.astype(jnp.bfloat16), ('sub', 'col'))  62.8 us
    all_gather x1, waiting for transfers between devices, local(): lax.all_gather(leaf_forward, 'row', axis=0, tiled=True)[None]  41.5 us
  transfers between devices with their start and end apart: 3, of which 2 were waited for; matrix products, arithmetic and copies ran while one was open for 1% of the time, Pallas kernels for 0%

profile of v1, /device:TPU:4, one launch (start us, length us, event | category | flops | bytes accessed | tf_op | source)
XLA Modules:
  0.0 1273.4 jit_solution(9164382989859401286)
XLA Ops:
  11.6 41.5 %all-gather.9.cloned.1.call-done = bf16[64,64,256]{2,1,0:T(8,128)(2,1)} async-done(((bf16[4,64,256]{2,1,0:T(8,128)(2,1)}), bf16[64,64,256]{2,1,0:T(8,128)(2,1)}) %all-gather.9.cloned.1.call-update) | async-done | bytes 2097168 | tf_op jit(solution)/shard_map/all_gather | solution.py:33
  59.8 62.8 %psum.21 = bf16[1,64,256]{2,1,0:T(8,128)(2,1)S(1)} all-reduce(bf16[1,64,256]{2,1,0:T(8,128)(2,1)S(1)} %fusion.62), channel_id=1, replica_groups=mesh['sub'=4,'row'=16,'col'=4] {'sub','col'}, use_global_device_ids=true, to_apply=%region_0.1 | all-reduce | flops 16384 | bytes 65536 | tf_op jit(solution)/shard_map/psum | solution.py:39
  122.7 303.0 %while.34 = (s32[]{:T(128)}, f32[1,64,256]{2,1,0:T(8,128)S(1)}, bf16[16,64,256]{2,1,0:T(8,128)(2,1)S(1)}, s32[1]{0:T(128)}, bf16[1,16,256,256]{3,2,1,0:T(8,128)(...) while((s32[]{:T(128)}, f32[1,64,256]{2,1,0:T(8,128)S(1)}, ...), condition=%wide.region_3.4_spmd.clone, body=%wide.region_1.3_spmd.clone.sunk | while | flops 17317896 | bytes 1804486 | solution.py:67
  123.8 17.1 %all-gather.3 = bf16[1024,256]{1,0:T(8,128)(2,1)S(1)} all-gather(bf16[64,256]{1,0:T(8,128)(2,1)S(1)} %fusion.97), channel_id=2, replica_groups=mesh['sub'=4,'row'=16,'col'=4] {'row'}, dimensions={0}, use_global_device_ids=true | all-gather | bytes 557056 | tf_op jit(solution)/shard_map/while/body/eval_jaxpr/all_gather | solution.py:8
  143.3 16.0 %all-gather.3 = bf16[1024,256]{1,0:T(8,128)(2,1)S(1)} all-gather(bf16[64,256]{1,0:T(8,128)(2,1)S(1)} %fusion.97), channel_id=2, replica_groups=mesh['sub'=4,'row'=16,'col'=4] {'row'}, dimensions={0}, use_global_device_ids=true | all-gather | bytes 557056 | tf_op jit(solution)/shard_map/while/body/eval_jaxpr/all_gather | solution.py:8
  161.7 17.5 %all-gather.3 = bf16[1024,256]{1,0:T(8,128)(2,1)S(1)} all-gather(bf16[64,256]{1,0:T(8,128)(2,1)S(1)} %fusion.97), channel_id=2, replica_groups=mesh['sub'=4,'row'=16,'col'=4] {'row'}, dimensions={0}, use_global_device_ids=true | all-gather | bytes 557056 | tf_op jit(solution)/shard_map/while/body/eval_jaxpr/all_gather | solution.py:8
  199.8 17.2 %all-gather.3 = bf16[1024,256]{1,0:T(8,128)(2,1)S(1)} all-gather(bf16[64,256]{1,0:T(8,128)(2,1)S(1)} %fusion.97), channel_id=2, replica_groups=mesh['sub'=4,'row'=16,'col'=4] {'row'}, dimensions={0}, use_global_device_ids=true | all-gather | bytes 557056 | tf_op jit(solution)/shard_map/while/body/eval_jaxpr/all_gather | solution.py:8
  237.6 17.2 %all-gather.3 = bf16[1024,256]{1,0:T(8,128)(2,1)S(1)} all-gather(bf16[64,256]{1,0:T(8,128)(2,1)S(1)} %fusion.97), channel_id=2, replica_groups=mesh['sub'=4,'row'=16,'col'=4] {'row'}, dimensions={0}, use_global_device_ids=true | all-gather | bytes 557056 | tf_op jit(solution)/shard_map/while/body/eval_jaxpr/all_gather | solution.py:8
  257.2 15.9 %all-gather.3 = bf16[1024,256]{1,0:T(8,128)(2,1)S(1)} all-gather(bf16[64,256]{1,0:T(8,128)(2,1)S(1)} %fusion.97), channel_id=2, replica_groups=mesh['sub'=4,'row'=16,'col'=4] {'row'}, dimensions={0}, use_global_device_ids=true | all-gather | bytes 557056 | tf_op jit(solution)/shard_map/while/body/eval_jaxpr/all_gather | solution.py:8
  275.5 17.2 %all-gather.3 = bf16[1024,256]{1,0:T(8,128)(2,1)S(1)} all-gather(bf16[64,256]{1,0:T(8,128)(2,1)S(1)} %fusion.97), channel_id=2, replica_groups=mesh['sub'=4,'row'=16,'col'=4] {'row'}, dimensions={0}, use_global_device_ids=true | all-gather | bytes 557056 | tf_op jit(solution)/shard_map/while/body/eval_jaxpr/all_gather | solution.py:8
  295.0 15.9 %all-gather.3 = bf16[1024,256]{1,0:T(8,128)(2,1)S(1)} all-gather(bf16[64,256]{1,0:T(8,128)(2,1)S(1)} %fusion.97), channel_id=2, replica_groups=mesh['sub'=4,'row'=16,'col'=4] {'row'}, dimensions={0}, use_global_device_ids=true | all-gather | bytes 557056 | tf_op jit(solution)/shard_map/while/body/eval_jaxpr/all_gather | solution.py:8
  313.3 17.2 %all-gather.3 = bf16[1024,256]{1,0:T(8,128)(2,1)S(1)} all-gather(bf16[64,256]{1,0:T(8,128)(2,1)S(1)} %fusion.97), channel_id=2, replica_groups=mesh['sub'=4,'row'=16,'col'=4] {'row'}, dimensions={0}, use_global_device_ids=true | all-gather | bytes 557056 | tf_op jit(solution)/shard_map/while/body/eval_jaxpr/all_gather | solution.py:8
  351.1 17.2 %all-gather.3 = bf16[1024,256]{1,0:T(8,128)(2,1)S(1)} all-gather(bf16[64,256]{1,0:T(8,128)(2,1)S(1)} %fusion.97), channel_id=2, replica_groups=mesh['sub'=4,'row'=16,'col'=4] {'row'}, dimensions={0}, use_global_device_ids=true | all-gather | bytes 557056 | tf_op jit(solution)/shard_map/while/body/eval_jaxpr/all_gather | solution.py:8
  389.0 17.2 %all-gather.3 = bf16[1024,256]{1,0:T(8,128)(2,1)S(1)} all-gather(bf16[64,256]{1,0:T(8,128)(2,1)S(1)} %fusion.97), channel_id=2, replica_groups=mesh['sub'=4,'row'=16,'col'=4] {'row'}, dimensions={0}, use_global_device_ids=true | all-gather | bytes 557056 | tf_op jit(solution)/shard_map/while/body/eval_jaxpr/all_gather | solution.py:8
  425.8 767.1 %while.33 = (s32[]{:T(128)}, bf16[16,64,256]{2,1,0:T(8,128)(2,1)S(1)}, bf16[16,64,256]{2,1,0:T(8,128)(2,1)S(1)}, s32[]{:T(128)}, s32[1]{0:T(128)}, /*index=5*/bf...) while((s32[]{:T(128)}, ...), condition=%wide.region_6.7_spmd, body=%wide.region_4.6_spmd.sunk | while | flops 17039368 | bytes 494251 | solution.py:87
  426.8 47.2 %psum.23 = bf16[64,256]{1,0:T(8,128)(2,1)S(1)} all-reduce(bf16[64,256]{1,0:T(8,128)(2,1)S(1)} %convolution_convert_fusion.6), channel_id=1, replica_groups=mesh['sub'=4,'row'=16,'col'=4] {'row'}, use_global_device_ids=true, to_apply=%region_5.5 | all-reduce | flops 16384 | bytes 65536 | tf_op jit(solution)/shard_map/while/body/eval_jaxpr/psum | solution.py:80
  476.2 45.7 %psum.23 = bf16[64,256]{1,0:T(8,128)(2,1)S(1)} all-reduce(bf16[64,256]{1,0:T(8,128)(2,1)S(1)} %convolution_convert_fusion.6), channel_id=1, replica_groups=mesh['sub'=4,'row'=16,'col'=4] {'row'}, use_global_device_ids=true, to_apply=%region_5.5 | all-reduce | flops 16384 | bytes 65536 | tf_op jit(solution)/shard_map/while/body/eval_jaxpr/psum | solution.py:80
  524.0 45.7 %psum.23 = bf16[64,256]{1,0:T(8,128)(2,1)S(1)} all-reduce(bf16[64,256]{1,0:T(8,128)(2,1)S(1)} %convolution_convert_fusion.6), channel_id=1, replica_groups=mesh['sub'=4,'row'=16,'col'=4] {'row'}, use_global_device_ids=true, to_apply=%region_5.5 | all-reduce | flops 16384 | bytes 65536 | tf_op jit(solution)/shard_map/while/body/eval_jaxpr/psum | solution.py:80
  571.9 45.7 %psum.23 = bf16[64,256]{1,0:T(8,128)(2,1)S(1)} all-reduce(bf16[64,256]{1,0:T(8,128)(2,1)S(1)} %convolution_convert_fusion.6), channel_id=1, replica_groups=mesh['sub'=4,'row'=16,'col'=4] {'row'}, use_global_device_ids=true, to_apply=%region_5.5 | all-reduce | flops 16384 | bytes 65536 | tf_op jit(solution)/shard_map/while/body/eval_jaxpr/psum | solution.py:80
  619.7 45.7 %psum.23 = bf16[64,256]{1,0:T(8,128)(2,1)S(1)} all-reduce(bf16[64,256]{1,0:T(8,128)(2,1)S(1)} %convolution_convert_fusion.6), channel_id=1, replica_groups=mesh['sub'=4,'row'=16,'col'=4] {'row'}, use_global_device_ids=true, to_apply=%region_5.5 | all-reduce | flops 16384 | bytes 65536 | tf_op jit(solution)/shard_map/while/body/eval_jaxpr/psum | solution.py:80
  667.6 45.7 %psum.23 = bf16[64,256]{1,0:T(8,128)(2,1)S(1)} all-reduce(bf16[64,256]{1,0:T(8,128)(2,1)S(1)} %convolution_convert_fusion.6), channel_id=1, replica_groups=mesh['sub'=4,'row'=16,'col'=4] {'row'}, use_global_device_ids=true, to_apply=%region_5.5 | all-reduce | flops 16384 | bytes 65536 | tf_op jit(solution)/shard_map/while/body/eval_jaxpr/psum | solution.py:80
  715.4 45.7 %psum.23 = bf16[64,256]{1,0:T(8,128)(2,1)S(1)} all-reduce(bf16[64,256]{1,0:T(8,128)(2,1)S(1)} %convolution_convert_fusion.6), channel_id=1, replica_groups=mesh['sub'=4,'row'=16,'col'=4] {'row'}, use_global_device_ids=true, to_apply=%region_5.5 | all-reduce | flops 16384 | bytes 65536 | tf_op jit(solution)/shard_map/while/body/eval_jaxpr/psum | solution.py:80
  763.2 45.7 %psum.23 = bf16[64,256]{1,0:T(8,128)(2,1)S(1)} all-reduce(bf16[64,256]{1,0:T(8,128)(2,1)S(1)} %convolution_convert_fusion.6), channel_id=1, replica_groups=mesh['sub'=4,'row'=16,'col'=4] {'row'}, use_global_device_ids=true, to_apply=%region_5.5 | all-reduce | flops 16384 | bytes 65536 | tf_op jit(solution)/shard_map/while/body/eval_jaxpr/psum | solution.py:80
  811.1 45.7 %psum.23 = bf16[64,256]{1,0:T(8,128)(2,1)S(1)} all-reduce(bf16[64,256]{1,0:T(8,128)(2,1)S(1)} %convolution_convert_fusion.6), channel_id=1, replica_groups=mesh['sub'=4,'row'=16,'col'=4] {'row'}, use_global_device_ids=true, to_apply=%region_5.5 | all-reduce | flops 16384 | bytes 65536 | tf_op jit(solution)/shard_map/while/body/eval_jaxpr/psum | solution.py:80
  858.9 45.7 %psum.23 = bf16[64,256]{1,0:T(8,128)(2,1)S(1)} all-reduce(bf16[64,256]{1,0:T(8,128)(2,1)S(1)} %convolution_convert_fusion.6), channel_id=1, replica_groups=mesh['sub'=4,'row'=16,'col'=4] {'row'}, use_global_device_ids=true, to_apply=%region_5.5 | all-reduce | flops 16384 | bytes 65536 | tf_op jit(solution)/shard_map/while/body/eval_jaxpr/psum | solution.py:80
  906.8 45.7 %psum.23 = bf16[64,256]{1,0:T(8,128)(2,1)S(1)} all-reduce(bf16[64,256]{1,0:T(8,128)(2,1)S(1)} %convolution_convert_fusion.6), channel_id=1, replica_groups=mesh['sub'=4,'row'=16,'col'=4] {'row'}, use_global_device_ids=true, to_apply=%region_5.5 | all-reduce | flops 16384 | bytes 65536 | tf_op jit(solution)/shard_map/while/body/eval_jaxpr/psum | solution.py:80
  954.6 45.7 %psum.23 = bf16[64,256]{1,0:T(8,128)(2,1)S(1)} all-reduce(bf16[64,256]{1,0:T(8,128)(2,1)S(1)} %convolution_convert_fusion.6), channel_id=1, replica_groups=mesh['sub'=4,'row'=16,'col'=4] {'row'}, use_global_device_ids=true, to_apply=%region_5.5 | all-reduce | flops 16384 | bytes 65536 | tf_op jit(solution)/shard_map/while/body/eval_jaxpr/psum | solution.py:80
  1002.5 45.7 %psum.23 = bf16[64,256]{1,0:T(8,128)(2,1)S(1)} all-reduce(bf16[64,256]{1,0:T(8,128)(2,1)S(1)} %convolution_convert_fusion.6), channel_id=1, replica_groups=mesh['sub'=4,'row'=16,'col'=4] {'row'}, use_global_device_ids=true, to_apply=%region_5.5 | all-reduce | flops 16384 | bytes 65536 | tf_op jit(solution)/shard_map/while/body/eval_jaxpr/psum | solution.py:80
  1050.3 45.7 %psum.23 = bf16[64,256]{1,0:T(8,128)(2,1)S(1)} all-reduce(bf16[64,256]{1,0:T(8,128)(2,1)S(1)} %convolution_convert_fusion.6), channel_id=1, replica_groups=mesh['sub'=4,'row'=16,'col'=4] {'row'}, use_global_device_ids=true, to_apply=%region_5.5 | all-reduce | flops 16384 | bytes 65536 | tf_op jit(solution)/shard_map/while/body/eval_jaxpr/psum | solution.py:80
  1098.2 45.7 %psum.23 = bf16[64,256]{1,0:T(8,128)(2,1)S(1)} all-reduce(bf16[64,256]{1,0:T(8,128)(2,1)S(1)} %convolution_convert_fusion.6), channel_id=1, replica_groups=mesh['sub'=4,'row'=16,'col'=4] {'row'}, use_global_device_ids=true, to_apply=%region_5.5 | all-reduce | flops 16384 | bytes 65536 | tf_op jit(solution)/shard_map/while/body/eval_jaxpr/psum | solution.py:80
  1146.0 45.7 %psum.23 = bf16[64,256]{1,0:T(8,128)(2,1)S(1)} all-reduce(bf16[64,256]{1,0:T(8,128)(2,1)S(1)} %convolution_convert_fusion.6), channel_id=1, replica_groups=mesh['sub'=4,'row'=16,'col'=4] {'row'}, use_global_device_ids=true, to_apply=%region_5.5 | all-reduce | flops 16384 | bytes 65536 | tf_op jit(solution)/shard_map/while/body/eval_jaxpr/psum | solution.py:80
  1199.8 65.3 %reduce-scatter.2.cloned.1.call-done = bf16[4,64,256]{2,1,0:T(8,128)(2,1)} async-done(((bf16[64,64,256]{2,1,0:T(8,128)(2,1)}), bf16[4,64,256]{2,1,0:T(8,128)(2,1)}) %reduce-scatter.2.cloned.1.call-update) | async-done | bytes 131088 | tf_op jit(solution)/shard_map/reduce_scatter | solution.py:94
  (126 shorter events, 169.6 us)
Async XLA Ops:
  7.2 0.9 copy-start
  7.2 45.9 %all-gather.9.cloned.1.call-start = ((), (), s32[]{:S(2)}) async-start(), calls=%async_computation.2 | async-start | bytes 2228224 | tf_op jit(solution)/shard_map/all_gather | solution.py:33
  10.1 112.6 %all-gather.7.cloned.1.call-start = ((), (), s32[]{:S(2)}) async-start(), calls=%async_computation.1 | async-start | bytes 2621440 | tf_op jit(solution)/shard_map/all_gather | solution.py:41
  10.8 1254.3 %reduce-scatter.2.cloned.1.call-start = ((), (), s32[]{:S(2)}) async-start(), calls=%async_computation.3 | async-start | bytes 2228224 | tf_op jit(solution)/shard_map/reduce_scatter | solution.py:94
  1199.2 65.9 %copy-start.1 = (bf16[4,64,256]{2,1,0:T(8,128)(2,1)S(1)}, bf16[4,64,256]{2,1,0:T(8,128)(2,1)}, u32[]{:S(2)}) copy-start(bf16[4,64,256]{2,1,0:T(8,128)(2,1)} %fusion.50) | copy-start | bytes 393220
  1199.2 65.9 %copy-start.2 = (bf16[1,4,1,256,256]{4,3,2,1,0:T(8,128)(2,1)S(1)}, bf16[1,4,1,256,256]{4,3,2,1,0:T(8,128)(2,1)}, u32[]{:S(2)}) copy-start(bf16[1,4,1,256,256]{4,3,2,1,0:T(8,128)(2,1)} %param.12) | copy-start | bytes 1572868
Sparse Core Ops, SparseCore 0:
  10.4 42.6 all-gather.8
  54.9 32.1 all-gather.6
  1199.3 65.7 reduce-scatter.1
